TPU v7x, 32 devices: a whole 2x2x4 slice. The times are simulated.
32 devices in a mesh: src: 8 (over z, y), snk: 4 (over x, core).
Axes of the slice: x: 2, y: 2, z: 4, core: 2. Of those that a mesh axis runs over, the one named last changes fastest.
Arguments:
- tau_cols: bfloat16 [2, 8, 8, 256, 256], P(None, 'src', None, 'snk'), may hold values from -0.25 to 0.25
- elementals: bfloat16 [256, 2, 256, 256], P('src'), may hold values from -0.25 to 0.25
- need_ids: int32 [8, 8], replicated, may hold values from 0 to 255, as said below
- diagrams: int32 [8, 8, 3], P('src'), may hold values from 0 to 15, as said below
- phases: int32 [16], replicated, may hold values from 0 to 3
- block_sizes: int32 [4], replicated, may hold values from 1 to 3, 8 in all
Outputs:
- correlators: float32 [8, 4, 3, 2, 8], P('src', 'snk')
Inputs may be any that keep to these rules, and one draw needn't show every extreme that they name: `block_sizes`: the sizes sum to 8, and one of them is exactly 3. `need_ids`: the 8 ids of a row are distinct. `diagrams`: entry 0 of a diagram is below 4, entry 1 below 4, entry 2 below 16; each of a row's 4 sink-side and 4 source-side entries is named by some diagram of the row.
All inputs are finite; a program needn't handle non-finite values.
Results may differ from a plain program's by a relative error of at most 0.004.
Values may be sent and summed in bfloat16 or wider, within the bound.
A program may use at most 64 MiB of HBM per device.

v0:
```python
import jax
import jax.numpy as jnp
from jax import lax
from jax.sharding import PartitionSpec as P

NSN = 4
MAXB = 3


def slot_values(gathered, tau_slot, diagram_rows, phases):
    real_part = tau_slot[0]
    imag_part = tau_slot[1]
    left_stack = jnp.stack([jnp.stack([real_part, imag_part]), jnp.stack([-imag_part, real_part])])
    right_stack = jnp.stack([jnp.stack([real_part, -imag_part]), jnp.stack([imag_part, real_part])])
    left_node = lax.dot_general(
        gathered[:, :, :NSN],
        left_stack,
        (((1, 3), (0, 3)), ((), ())),
        preferred_element_type=jnp.float32,
    ).astype(jnp.bfloat16)
    right_node = lax.dot_general(
        gathered[:, :, NSN:],
        right_stack,
        (((1, 3), (0, 2)), ((), ())),
        preferred_element_type=jnp.float32,
    ).astype(jnp.bfloat16)
    pair_sums = lax.dot_general(
        left_node, right_node, (((0, 3), (3, 0)), ((), ())), preferred_element_type=jnp.float32
    )
    pair_real = pair_sums[:, 0, :, 0] - pair_sums[:, 1, :, 1]
    pair_imag = pair_sums[:, 0, :, 1] + pair_sums[:, 1, :, 0]
    sink_pick = (
        diagram_rows[:, 0:1] == jnp.arange(pair_real.shape[0], dtype=jnp.int32)[None, :]
    ).astype(jnp.float32)
    source_pick = (
        diagram_rows[:, 1:2] == jnp.arange(pair_real.shape[1], dtype=jnp.int32)[None, :]
    ).astype(jnp.float32)
    chosen_real = jnp.sum(
        sink_pick[:, :, None] * pair_real[None] * source_pick[:, None, :], axis=(1, 2)
    )
    chosen_imag = jnp.sum(
        sink_pick[:, :, None] * pair_imag[None] * source_pick[:, None, :], axis=(1, 2)
    )
    gamma_pick = diagram_rows[:, 2:3] == jnp.arange(phases.shape[0], dtype=jnp.int32)[None, :]
    quarter = jnp.sum(jnp.where(gamma_pick, phases[None, :], 0), axis=1)
    cosine = (quarter == 0).astype(jnp.float32) - (quarter == 2).astype(jnp.float32)
    sine_part = (quarter == 1).astype(jnp.float32) - (quarter == 3).astype(jnp.float32)
    return jnp.stack(
        [
            cosine * chosen_real - sine_part * chosen_imag,
            sine_part * chosen_real + cosine * chosen_imag,
        ]
    )


def local(tau_cols, elementals, need_ids, diagrams, phases, block_sizes):
    groups = lax.axis_size("snk")
    column = lax.axis_index("snk")
    full_width = tau_cols.shape[4]
    col_count = tau_cols.shape[3]
    sink_count = tau_cols.shape[2]
    diagram_rows = diagrams[0]
    starts = jnp.cumsum(block_sizes) - block_sizes
    offsets = jnp.arange(MAXB, dtype=jnp.int32)
    picked = jnp.take(elementals, need_ids, axis=2)
    arrived = lax.all_to_all(picked, "src", split_axis=2, concat_axis=0, tiled=True)
    gathered = arrived.reshape(full_width, 2, need_ids.shape[1], full_width)
    local_tau = tau_cols[:, 0]
    per_group = sink_count // groups
    half_turn = groups // 2
    packed = local_tau.reshape(2, groups, per_group, col_count, full_width)
    packed = jnp.roll(packed, -half_turn, axis=1)
    arrived_tau = lax.all_to_all(packed, "snk", split_axis=1, concat_axis=3, tiled=True)
    blocks = arrived_tau.reshape(2, per_group, full_width, full_width)
    results = jnp.stack(
        [
            slot_values(gathered, blocks[:, place], diagram_rows, phases)
            for place in range(per_group)
        ]
    )
    all_values = lax.all_gather(results, "snk", axis=0, tiled=True)
    all_values = jnp.roll(all_values, half_turn * per_group, axis=0)
    own_start = lax.dynamic_index_in_dim(starts, column, keepdims=False)
    own_size = lax.dynamic_index_in_dim(block_sizes, column, keepdims=False)
    own_filled = offsets < own_size
    own_times = jnp.where(own_filled, own_start + offsets, 0)
    correlators = jnp.take(all_values, own_times, axis=0) * own_filled[:, None, None].astype(
        jnp.float32
    )
    return correlators.reshape(1, 1, MAXB, 2, diagram_rows.shape[0])


def solution(mesh):
    placed = (
        P(None, "src", None, "snk", None),
        P("src", None, None, None),
        P(),
        P("src", None, None),
        P(),
        P(),
    )
    return jax.shard_map(
        local,
        mesh=mesh,
        in_specs=placed,
        out_specs=P("src", "snk", None, None, None),
        check_vma=False,
    )
```

profile of v0, /device:TPU:0, one launch (start us, length us, event | category | flops | bytes accessed | tf_op | source)
XLA Modules:
  0.0 94.8 jit_solution(11811888920916635707)
XLA Ops:
  0.0 0.0 copy-start.6
  0.0 1.1 %fusion.38 = (bf16[2,2,2,64,256]{4,3,2,1,0:T(8,128)(2,1)S(1)}, bf16[2,2,2,64,256]{4,3,2,1,0:T(8,128)(2,1)S(1)}) fusion(bf16[2,4,2,64,256]{4,3,2,1,0:T(8,128)(2,1)} %bitcast.147), kind=kLoop, calls=%fused_computation.106 | loop fusion | bytes 1048576 | tf_op jit(solution)/shard_map/jit(_roll_static)/slice | solution.py:72
  1.1 0.9 copy.35
  2.0 4.2 %all-to-all-start.1 = ((bf16[2,4,2,64,256]{4,3,2,0,1:T(8,128)(2,1)}), bf16[2,4,2,64,256]{4,3,2,0,1:T(8,128)(2,1)S(1)}, u32[]{:S(2)}, u32[]{:S(2)}) async-start(bf16[2,4,2,64,256]{4,3,2,0,1:T(8,128)(2,1)} %copy.35), calls=%async_computation.1 | async-start | bytes 1048576 | tf_op jit(solution)/shard_map/all_to_all | solution.py:73
  6.2 0.0 copy-done.6
  6.3 0.1 reshape.341
  6.4 6.2 %gather_fusion = bf16[64,32,2,256]{3,0,2,1:T(8,128)(2,1)S(1)} fusion(bf16[32,2,256,256]{3,2,1,0:T(8,128)(2,1)} %param.7, s32[1024]{0:T(1024)S(1)} %pad_clamp_fusion.1), kind=kCustom, calls=%fused_computation | custom fusion | bytes 4194560 | tf_op jit(solution)/shard_map/jit(_take)/gather | solution.py:65
  12.5 2.1 %fusion = bf16[32,2,8,8,256]{4,3,1,0,2:T(8,128)(2,1)} fusion(pred[8,8]{1,0:T(8,128)(4,1)S(1)} %compare_and_fusion, bf16[64,32,2,256]{3,0,2,1:T(8,128)(2,1)S(1)} %gather_fusion), kind=kLoop, calls=%fused_computation.7 | loop fusion | flops 1048576 | bytes 4194368 | tf_op jit(solution)/shard_map/jit(_take)/select_n | solution.py:65
  14.7 0.0 copy-start.7
  14.7 0.0 copy-start.8
  14.7 0.0 copy-start.9
  14.7 0.4 all-to-all-done.1
  15.1 6.5 %all-to-all-start = ((bf16[32,2,8,8,256]{4,3,1,0,2:T(8,128)(2,1)}), bf16[32,2,8,8,256]{4,3,1,0,2:T(8,128)(2,1)S(1)}, u32[]{:S(2)}, u32[]{:S(2)}) async-start(bf16[32,2,8,8,256]{4,3,1,0,2:T(8,128)(2,1)} %fusion), calls=%async_computation | async-start | bytes 4194304 | tf_op jit(solution)/shard_map/all_to_all | solution.py:66
  21.6 0.0 copy-done.7
  21.6 0.0 copy-done.8
  21.6 0.2 reduce-window.9
  21.8 0.6 dynamic_slice.7
  22.4 0.6 dynamic_slice.8
  23.0 1.3 %fusion.32 = s32[3]{0:T(128)S(1)} fusion(s32[]{:T(128)} %bitcast.3, s32[]{:T(128)} %bitcast), kind=kLoop, calls=%fused_computation.97 | loop fusion | flops 18 | bytes 20 | tf_op jit(solution)/shard_map/jit(_take)/jit(_where)/select_n | solution.py:87
  24.3 1.3 %compare_and_fusion.1 = (pred[3]{0:T(512)(128)(4,1)S(1)}, f32[3]{0:T(128)S(1)}) fusion(s32[]{:T(128)} %bitcast.3, s32[]{:T(128)} %bitcast), kind=kLoop, calls=%fused_computation.85 | loop fusion | flops 30 | bytes 23 | tf_op jit(solution)/shard_map/jit(_take)/and | solution.py:87
  25.6 0.0 copy-done.9
  25.6 0.2 select_reduce_fusion
  25.9 1.3 %fusion.17 = (bf16[1,2,256,256]{3,2,0,1:T(8,128)(2,1)S(1)}, bf16[1,2,256,256]{3,2,1,0:T(8,128)(2,1)}, bf16[1,2,256,256]{3,2,1,0:T(8,128)(2,1)}, bf16[1,2,256,256...) fusion(bf16[1,256,256]{2,1,0:T(8,128)(2,1)S(1)} %get-tuple-elem, ...), kind=kLoop, calls=%fused_computation.41 | loop fusion | flops 1048576 | bytes 2883584 | tf_op jit(solution)/shard_map/stack | solution.py:13
  27.2 43.1 %all-to-all-done = bf16[32,2,8,8,256]{4,3,1,0,2:T(8,128)(2,1)S(1)} async-done(((bf16[32,2,8,8,256]{4,3,1,0,2:T(8,128)(2,1)}), bf16[32,2,8,8,256]{4,3,1,0,2:T(8,128)(2,1)S(1)}, u32[]{:S(2)}, u32[]{:S(2)}) %all-to-all-start) | async-done | bytes 2097184 | tf_op jit(solution)/shard_map/all_to_all | solution.py:66
  70.2 0.0 copy-start.4
  70.2 0.0 copy-start.5
  70.2 0.7 fusion.37
  70.9 0.0 copy-start
  70.9 1.0 %copy-done = bf16[256,2,4,256]{3,2,1,0:T(4,128)(2,1)} copy-done((bf16[256,2,4,256]{3,2,1,0:T(4,128)(2,1)}, bf16[256,2,4,256]{3,2,1,0:T(4,128)(2,1)S(1)}, u32[]{:S(2)}) %copy-start) | copy-done | bytes 1048600
  71.9 0.0 copy-done.4
  71.9 0.0 copy-done.5
  71.9 0.7 bitcast_convert_fusion.2
  72.6 0.7 copy.41
  73.3 1.8 %fusion.1 = bf16[256,4,2,256,1]{3,0,2,1,4:T(8,128)(2,1)S(1)} fusion(bf16[256,2,4,256]{3,2,1,0:T(4,128)(2,1)S(1)} %get-tuple-element.9, bf16[1,2,256,256]{3,2,0,1:T(8,128)(2,1)} %get-tuple-element.48, bf16[1,2,256,256]{3,2,0,1:T(8,128)(2,1)} %get-tuple-element.51), kind=kOutput, calls=%fused_computation.8 | convolution fusion | flops 538443776 | bytes 2621440 | tf_op jit(solution)/shard_map/dot_general | solution.py:15
  75.1 0.0 copy-start.1
  75.1 0.0 copy-start.2
  75.1 0.0 copy-start.3
  75.1 4.9 %convolution_bitcast_fusion.1 = f32[4,2,4,2]{2,0,3,1:T(4,128)S(1)} fusion(bf16[256,4,2,256]{0,1,3,2:T(4,128)(2,1)S(1)} %copy.41, bf16[256,4,2,256,1]{3,0,2,1,4:T(8,128)(2,1)S(1)} %fusion.1), kind=kOutput, calls=%fused_computation.11 | convolution fusion | flops 8388608 | bytes 2097408 | tf_op jit(solution)/shard_map/dot_general | solution.py:27
  80.1 0.0 copy-done.1
  80.1 0.0 copy-done.2
  80.1 0.0 copy-done.3
  80.1 0.7 bitcast_convert_fusion
  80.8 0.7 copy.45
  81.5 1.7 %fusion.2 = bf16[256,4,2,256,1]{3,0,2,1,4:T(8,128)(2,1)S(1)} fusion(bf16[256,2,4,256]{3,2,1,0:T(4,128)(2,1)S(1)} %get-tuple-element.9, bf16[1,2,256,256]{3,2,0,1:T(8,128)(2,1)} %get-tuple-element.28, bf16[1,2,256,256]{3,2,0,1:T(8,128)(2,1)S(1)} %get-tuple-element.19), kind=kOutput, calls=%fused_computation.9 | convolution fusion | flops 538443776 | bytes 2621440 | tf_op jit(solution)/shard_map/dot_general | solution.py:15
  83.2 4.9 %convolution_bitcast_fusion = f32[4,2,4,2]{2,0,3,1:T(4,128)S(1)} fusion(bf16[256,4,2,256]{0,1,3,2:T(4,128)(2,1)S(1)} %copy.45, bf16[256,4,2,256,1]{3,0,2,1,4:T(8,128)(2,1)S(1)} %fusion.2), kind=kOutput, calls=%fused_computation.10 | convolution fusion | flops 8388608 | bytes 2097408 | tf_op jit(solution)/shard_map/dot_general | solution.py:27
  88.2 0.1 multiply_reduce_fusion.3
  88.4 5.2 %all_gather.3 = f32[8,2,8]{2,1,0:T(2,128)S(1)} all-gather(f32[2,2,8]{2,1,0:T(2,128)S(1)} %pad_maximum_fusion.12), channel_id=1, replica_groups=mesh['src'=8,'snk'=4] {'snk'}, dimensions={0}, use_global_device_ids=true | all-gather | bytes 640 | tf_op jit(solution)/shard_map/all_gather | solution.py:81
  93.6 0.6 gather_fusion.1
  94.1 0.7 fusion.23
  (20 shorter events, 0.2 us)
Async XLA Ops:
  0.0 6.2 %copy-start.6 = (s32[8,8]{1,0:T(8,128)S(1)}, s32[8,8]{1,0:T(8,128)}, u32[]{:S(2)}) copy-start(s32[8,8]{1,0:T(8,128)} %param.8) | copy-start | bytes 772
  2.0 13.1 %all-to-all-start.1 = ((bf16[2,4,2,64,256]{4,3,2,0,1:T(8,128)(2,1)}), bf16[2,4,2,64,256]{4,3,2,0,1:T(8,128)(2,1)S(1)}, u32[]{:S(2)}, u32[]{:S(2)}) async-start(bf16[2,4,2,64,256]{4,3,2,0,1:T(8,128)(2,1)} %copy.35), calls=%async_computation.1 | async-start | bytes 1048576 | tf_op jit(solution)/shard_map/all_to_all | solution.py:73
  14.7 6.9 %copy-start.7 = (s32[1,8,3]{1,0,2:T(1,128)S(1)}, s32[1,8,3]{1,0,2:T(1,128)}, u32[]{:S(2)}) copy-start(s32[1,8,3]{1,0,2:T(1,128)} %param.9) | copy-start | bytes 292
  14.7 6.9 %copy-start.8 = (s32[4]{0:T(128)S(1)}, s32[4]{0:T(128)}, u32[]{:S(2)}) copy-start(s32[4]{0:T(128)} %param.11) | copy-start | bytes 52
  14.7 10.9 %copy-start.9 = (s32[16]{0:T(128)S(1)}, s32[16]{0:T(128)}, u32[]{:S(2)}) copy-start(s32[16]{0:T(128)} %param.10) | copy-start | bytes 196
  15.1 55.2 %all-to-all-start = ((bf16[32,2,8,8,256]{4,3,1,0,2:T(8,128)(2,1)}), bf16[32,2,8,8,256]{4,3,1,0,2:T(8,128)(2,1)S(1)}, u32[]{:S(2)}, u32[]{:S(2)}) async-start(bf16[32,2,8,8,256]{4,3,1,0,2:T(8,128)(2,1)} %fusion), calls=%async_computation | async-start | bytes 4194304 | tf_op jit(solution)/shard_map/all_to_all | solution.py:66
  70.2 1.7 %copy-start.4 = (bf16[1,2,256,256]{3,2,1,0:T(8,128)(2,1)S(1)}, bf16[1,2,256,256]{3,2,1,0:T(8,128)(2,1)}, u32[]{:S(2)}) copy-start(bf16[1,2,256,256]{3,2,1,0:T(8,128)(2,1)} %get-tuple-element.49) | copy-start | bytes 786436
  70.2 1.7 %copy-start.5 = (bf16[1,2,256,256]{3,2,1,0:T(8,128)(2,1)S(1)}, bf16[1,2,256,256]{3,2,1,0:T(8,128)(2,1)}, u32[]{:S(2)}) copy-start(bf16[1,2,256,256]{3,2,1,0:T(8,128)(2,1)} %get-tuple-element.50) | copy-start | bytes 786436
  70.9 1.0 %copy-start = (bf16[256,2,4,256]{3,2,1,0:T(4,128)(2,1)}, bf16[256,2,4,256]{3,2,1,0:T(4,128)(2,1)S(1)}, u32[]{:S(2)}) copy-start(bf16[256,2,4,256]{3,2,1,0:T(4,128)(2,1)S(1)} %get-tuple-element.10) | copy-start | bytes 3145732
  75.1 5.0 %copy-start.1 = (bf16[256,2,4,256]{3,2,1,0:T(4,128)(2,1)S(1)}, bf16[256,2,4,256]{3,2,1,0:T(4,128)(2,1)}, u32[]{:S(2)}) copy-start(bf16[256,2,4,256]{3,2,1,0:T(4,128)(2,1)} %copy-done) | copy-start | bytes 3145732
  75.1 5.0 %copy-start.2 = (bf16[1,2,256,256]{3,2,1,0:T(8,128)(2,1)S(1)}, bf16[1,2,256,256]{3,2,1,0:T(8,128)(2,1)}, u32[]{:S(2)}) copy-start(bf16[1,2,256,256]{3,2,1,0:T(8,128)(2,1)} %get-tuple-element.20) | copy-start | bytes 786436
  75.1 5.0 %copy-start.3 = (bf16[1,2,256,256]{3,2,1,0:T(8,128)(2,1)S(1)}, bf16[1,2,256,256]{3,2,1,0:T(8,128)(2,1)}, u32[]{:S(2)}) copy-start(bf16[1,2,256,256]{3,2,1,0:T(8,128)(2,1)} %get-tuple-element.27) | copy-start | bytes 786436
where the time goes:
time: 95.2 us; the launch traced here: 94.8 us
  waiting for transfers between devices  43.5 us (46%)
  matrix products  14.7 us (15%)
  local copies, waits for them, and re-layouts  13.2 us (14%)
  starting transfers between devices  10.8 us (11%)
  other arithmetic  7.21 us (8%)
  blocking collectives  5.19 us (5%)
    all_to_all x1, waiting for transfers between devices, local(): lax.all_to_all(picked, 'src', split_axis=2, concat_axis=0, tiled=True)  43.1 us
    dot_general x2, matrix products, slot_values(): lax.dot_general(left_node, right_node, (((0, 3), (3, 0)), ((), ())), pref...  9.84 us
    all_to_all x1, starting transfers between devices, local(): lax.all_to_all(picked, 'src', split_axis=2, concat_axis=0, tiled=True)  6.52 us
    gather x1, local copies, waits for them, and re-layouts, local(): picked = jnp.take(elementals, need_ids, axis=2)  6.18 us
    all_gather x1, blocking collectives, local(): all_values = lax.all_gather(results, 'snk', axis=0, tiled=True)  5.19 us
    all_to_all x1, starting transfers between devices, local(): lax.all_to_all(packed, 'snk', split_axis=1, concat_axis=3, tiled=True)  4.24 us
    dot_general x2, matrix products, slot_values(): lax.dot_general(gathered[:, :, :NSN], left_stack, (((1, 3), (0, 3)), ((),...  3.47 us
    select_n x2, other arithmetic, local(): picked = jnp.take(elementals, need_ids, axis=2)  2.12 us
  transfers between devices with their start and end apart: 2, of which 2 were waited for; matrix products, arithmetic and copies ran while one was open for 15% of the time, Pallas kernels for 0%

commit v1 on v0

--- a/solution.py
+++ b/solution.py
@@ -63,7 +63,12 @@
     starts = jnp.cumsum(block_sizes) - block_sizes
     offsets = jnp.arange(MAXB, dtype=jnp.int32)
     picked = jnp.take(elementals, need_ids, axis=2)
-    arrived = lax.all_to_all(picked, "src", split_axis=2, concat_axis=0, tiled=True)
+    arrived = jnp.concatenate(
+        lax.all_to_all(
+            jnp.stack(jnp.split(picked, lax.axis_size("src"), axis=2), axis=0), "src", 0, 0
+        ),
+        axis=0,
+    )
     gathered = arrived.reshape(full_width, 2, need_ids.shape[1], full_width)
     local_tau = tau_cols[:, 0]
     per_group = sink_count // groups

time: 95.2 us -> 103 us (1.082)
  local copies, waits for them, and re-layouts: 13.2 us -> 16.6 us
  waiting for transfers between devices: 43.5 us -> 46.2 us
  matrix products: 14.7 us -> 16.7 us
  other arithmetic: 7.21 us -> 6.14 us
    all_to_all x1, waiting for transfers between devices: 43.1 us -> 46.2 us  [local(): lax.all_to_all(jnp.stack(jnp.split(picked, lax.axis_size('src'), axis=2),...]
    convert_element_type x2, local copies, waits for them, and re-layouts: 1.42 us -> 3.49 us  [slot_values(): right_node = lax.dot_general(gathered[:, :, NSN:], right_stack, (((1, 3),...]
    dot_general x2, matrix products: 1.42 us -> 3.38 us  [slot_values(): lax.dot_general(gathered[:, :, NSN:], right_stack, (((1, 3), (0, 2)), (()...]
    unnamed x21 -> x26, local copies, waits for them, and re-layouts: 0.99 us -> 2.91 us
  transfers between devices with their start and end apart: 2 -> 2, of which waited for: 2 -> 1; matrix products, arithmetic and copies ran while one was open for 15% -> 13% of each run, Pallas kernels for 0% -> 0%
where the time goes in v1:
time: 103 us; the launch traced here: 102 us
  waiting for transfers between devices  46.2 us (45%)
  matrix products  16.7 us (16%)
  local copies, waits for them, and re-layouts  16.6 us (16%)
  starting transfers between devices  10.9 us (11%)
  other arithmetic  6.14 us (6%)
  blocking collectives  5.19 us (5%)
    all_to_all x1, waiting for transfers between devices, local(): lax.all_to_all(jnp.stack(jnp.split(picked, lax.axis_size('src'), axis=2),...  46.2 us
    dot_general x2, matrix products, slot_values(): lax.dot_general(left_node, right_node, (((0, 3), (3, 0)), ((), ())), pref...  9.85 us
    all_to_all x1, starting transfers between devices, local(): lax.all_to_all(jnp.stack(jnp.split(picked, lax.axis_size('src'), axis=2),...  6.7 us
    gather x1, local copies, waits for them, and re-layouts, local(): picked = jnp.take(elementals, need_ids, axis=2)  6.18 us
    all_gather x1, blocking collectives, local(): all_values = lax.all_gather(results, 'snk', axis=0, tiled=True)  5.19 us
    all_to_all x1, starting transfers between devices, local(): lax.all_to_all(packed, 'snk', split_axis=1, concat_axis=3, tiled=True)  4.24 us
    convert_element_type x2, local copies, waits for them, and re-layouts, slot_values(): right_node = lax.dot_general(gathered[:, :, NSN:], right_stack, (((1, 3),...  3.49 us
    dot_general x2, matrix products, slot_values(): lax.dot_general(gathered[:, :, :NSN], left_stack, (((1, 3), (0, 3)), ((),...  3.45 us
  transfers between devices with their start and end apart: 2, of which 1 were waited for; matrix products, arithmetic and copies ran while one was open for 13% of the time, Pallas kernels for 0%

profile of v1, /device:TPU:0, one launch (start us, length us, event | category | flops | bytes accessed | tf_op | source)
XLA Modules:
  0.0 102.1 jit_solution(13366572188466838303)
XLA Ops:
  0.0 0.0 copy-start.5
  0.0 0.0 copy-start.7
  0.0 1.1 %fusion.45 = (bf16[2,2,2,64,256]{4,3,2,1,0:T(8,128)(2,1)S(1)}, bf16[2,2,2,64,256]{4,3,2,1,0:T(8,128)(2,1)S(1)}) fusion(bf16[2,4,2,64,256]{4,3,2,1,0:T(8,128)(2,1)} %bitcast.177), kind=kLoop, calls=%fused_computation.121 | loop fusion | bytes 1048576 | tf_op jit(solution)/shard_map/jit(_roll_static)/slice | solution.py:77
  1.2 0.9 copy.52
  2.0 4.2 %all-to-all-start.1 = ((bf16[2,4,2,64,256]{4,3,2,0,1:T(8,128)(2,1)}), bf16[2,4,2,64,256]{4,3,2,0,1:T(8,128)(2,1)S(1)}, u32[]{:S(2)}, u32[]{:S(2)}) async-start(bf16[2,4,2,64,256]{4,3,2,0,1:T(8,128)(2,1)} %copy.52), calls=%async_computation.1 | async-start | bytes 1048576 | tf_op jit(solution)/shard_map/all_to_all | solution.py:78
  6.3 0.0 copy-done.5
  6.3 0.0 copy-done.7
  6.3 0.2 reduce-window.9
  6.5 0.6 dynamic_slice.7
  7.1 0.6 dynamic_slice.8
  7.7 0.1 reshape.336
  7.7 1.2 %fusion.40 = s32[3]{0:T(128)S(1)} fusion(s32[]{:T(128)} %bitcast.3, s32[]{:T(128)} %bitcast), kind=kLoop, calls=%fused_computation.113 | loop fusion | flops 18 | bytes 20 | tf_op jit(solution)/shard_map/jit(_take)/jit(_where)/select_n | solution.py:92
  9.0 6.2 %gather_fusion = bf16[64,32,2,256]{3,0,2,1:T(8,128)(2,1)S(1)} fusion(bf16[32,2,256,256]{3,2,1,0:T(8,128)(2,1)} %param.7, s32[1024]{0:T(1024)S(1)} %get-tuple-element.47), kind=kCustom, calls=%fused_computation | custom fusion | bytes 4194560 | tf_op jit(solution)/shard_map/jit(_take)/gather | solution.py:65
  15.2 1.3 %fusion = bf16[32,2,8,8,256]{4,0,1,3,2:T(8,128)(2,1)S(1)} fusion(bf16[8,8,32,2,256]{4,1,0,3,2:T(8,128)(2,1)S(1)} %bitcast.170, pred[8,8]{1,0:T(8,128)(4,1)S(1)} %compare_and_fusion), kind=kLoop, calls=%fused_computation.7 | loop fusion | flops 1048576 | bytes 4194368 | tf_op jit(solution)/shard_map/jit(_take)/select_n | solution.py:65
  16.7 0.0 copy-start
  16.7 1.3 %copy-done = bf16[8,32,2,1,8,256]{5,1,2,4,3,0:T(8,128)(2,1)} copy-done((bf16[8,32,2,1,8,256]{5,1,2,4,3,0:T(8,128)(2,1)}, bf16[8,32,2,1,8,256]{5,1,2,4,3,0:T(8,128)(2,1)S(1)}, u32[]{:S(2)}) %copy-start) | copy-done | bytes 2097176
  18.0 0.0 copy-start.6
  18.0 0.0 copy-start.8
  18.0 0.0 all-to-all-done.1
  18.0 6.7 %all-to-all-start = ((bf16[8,32,2,1,8,256]{5,1,2,4,3,0:T(8,128)(2,1)}), bf16[8,32,2,1,8,256]{5,1,2,4,3,0:T(8,128)(2,1)S(1)}, u32[]{:S(2)}, u32[]{:S(2)}) async-start(bf16[8,32,2,1,8,256]{5,1,2,4,3,0:T(8,128)(2,1)} %copy-done), calls=%async_computation | async-start | bytes 4194304 | tf_op jit(solution)/shard_map/all_to_all | solution.py:67
  24.7 0.0 copy-done.6
  24.7 1.2 %compare_and_fusion.1 = (pred[3]{0:T(512)(128)(4,1)S(1)}, f32[3]{0:T(128)S(1)}) fusion(s32[]{:T(128)} %bitcast.3, s32[]{:T(128)} %bitcast), kind=kLoop, calls=%fused_computation.101 | loop fusion | flops 30 | bytes 23 | tf_op jit(solution)/shard_map/jit(_take)/and | solution.py:92
  26.0 0.0 copy-done.8
  26.0 0.2 select_reduce_fusion
  26.3 1.1 %fusion.17 = (bf16[1,2,256,256]{3,2,0,1:T(8,128)(2,1)}, bf16[1,2,256,256]{3,2,1,0:T(8,128)(2,1)S(1)}, bf16[1,2,256,256]{3,2,1,0:T(8,128)(2,1)S(1)}, bf16[1,2,256...) fusion(bf16[1,256,256]{2,1,0:T(8,128)(2,1)S(1)} %get-tuple-elem, ...), kind=kLoop, calls=%fused_computation.41 | loop fusion | flops 1048576 | bytes 2883584 | tf_op jit(solution)/shard_map/stack | solution.py:13
  27.4 46.2 %all-to-all-done = bf16[8,32,2,1,8,256]{5,1,2,4,3,0:T(8,128)(2,1)S(1)} async-done(((bf16[8,32,2,1,8,256]{5,1,2,4,3,0:T(8,128)(2,1)}), bf16[8,32,2,1,8,256]{5,1,2,4,3,0:T(8,128)(2,1)S(1)}, u32[]{:S(2)}, u32[]{:S(2)}) %all-to-all-start) | async-done | bytes 2097184 | tf_op jit(solution)/shard_map/all_to_all | solution.py:67
  73.6 0.2 copy.51
  73.8 0.0 copy-start.1
  73.8 1.3 %copy-done.1 = bf16[8,32,2,1,8,256]{5,1,0,2,4,3:T(8,128)(2,1)} copy-done((bf16[8,32,2,1,8,256]{5,1,0,2,4,3:T(8,128)(2,1)}, bf16[8,32,2,1,8,256]{5,1,0,2,4,3:T(8,128)(2,1)S(1)}, u32[]{:S(2)}) %copy-start.1) | copy-done | bytes 2097176
  75.1 1.7 %bitcast_convert_fusion = bf16[256,4,2,256]{3,0,2,1:T(8,128)(2,1)} fusion(bf16[256,2,8,256]{3,0,1,2:T(8,128)(2,1)S(1)} %bitcast.173, bf16[1,2,256,256]{3,2,1,0:T(8,128)(2,1)S(1)} %get-tuple-element.18, bf16[1,2,256,256]{3,2,1,0:T(8,128)(2,1)S(1)} %get-tuple-element.25), kind=kOutput, calls=%fused_computation.2 | convolution fusion | flops 537657344 | bytes 2621440 | tf_op jit(solution)/shard_map/dot_general | solution.py:21
  76.8 0.0 copy-start.2
  76.8 1.8 %copy.61 = bf16[256,4,2,256]{0,1,3,2:T(4,128)(2,1)S(1)} copy(bf16[256,4,2,256]{3,0,2,1:T(8,128)(2,1)} %bitcast_convert_fusion) | data formatting | bytes 2097152 | tf_op jit(solution)/shard_map/convert_element_type | solution.py:26
  78.6 0.1 copy-done.2
  78.7 1.8 %fusion.2 = bf16[256,4,2,256,1]{3,0,2,1,4:T(8,128)(2,1)S(1)} fusion(bf16[256,2,8,256]{3,0,1,2:T(8,128)(2,1)S(1)} %bitcast.174, bf16[1,2,256,256]{3,2,0,1:T(8,128)(2,1)} %get-tuple-element.26, bf16[1,2,256,256]{3,2,0,1:T(8,128)(2,1)} %get-tuple-element.17), kind=kOutput, calls=%fused_computation.9 | convolution fusion | flops 538443776 | bytes 2621440 | tf_op jit(solution)/shard_map/dot_general | solution.py:15
  80.5 0.0 copy-start.3
  80.5 0.0 copy-start.4
  80.5 4.9 %convolution_bitcast_fusion = f32[4,2,4,2]{2,0,3,1:T(4,128)S(1)} fusion(bf16[256,4,2,256]{0,1,3,2:T(4,128)(2,1)S(1)} %copy.61, bf16[256,4,2,256,1]{3,0,2,1,4:T(8,128)(2,1)S(1)} %fusion.2), kind=kOutput, calls=%fused_computation.10 | convolution fusion | flops 8388608 | bytes 2097408 | tf_op jit(solution)/shard_map/dot_general | solution.py:27
  85.5 0.0 copy-done.3
  85.5 0.0 copy-done.4
  85.5 1.7 %bitcast_convert_fusion.2 = bf16[256,4,2,256]{3,0,2,1:T(8,128)(2,1)} fusion(bf16[256,2,8,256]{3,0,1,2:T(8,128)(2,1)S(1)} %bitcast.175, bf16[1,2,256,256]{3,2,1,0:T(8,128)(2,1)S(1)} %copy-done.4, bf16[1,2,256,256]{3,2,1,0:T(8,128)(2,1)S(1)} %copy-done.3), kind=kOutput, calls=%fused_computation.4 | convolution fusion | flops 537657344 | bytes 2621440 | tf_op jit(solution)/shard_map/dot_general | solution.py:21
  87.2 1.7 %copy.57 = bf16[256,4,2,256]{0,1,3,2:T(4,128)(2,1)S(1)} copy(bf16[256,4,2,256]{3,0,2,1:T(8,128)(2,1)} %bitcast_convert_fusion.2) | data formatting | bytes 2097152 | tf_op jit(solution)/shard_map/convert_element_type | solution.py:26
  88.8 1.7 %fusion.1 = bf16[256,4,2,256,1]{3,0,2,1,4:T(8,128)(2,1)S(1)} fusion(bf16[256,2,8,256]{3,0,1,2:T(8,128)(2,1)S(1)} %bitcast.176, bf16[1,2,256,256]{3,2,0,1:T(8,128)(2,1)S(1)} %get-tuple-element.48, bf16[1,2,256,256]{3,2,0,1:T(8,128)(2,1)} %get-tuple-element.51), kind=kOutput, calls=%fused_computation.8 | convolution fusion | flops 538443776 | bytes 2621440 | tf_op jit(solution)/shard_map/dot_general | solution.py:15
  90.5 4.9 %convolution_bitcast_fusion.1 = f32[4,2,4,2]{2,0,3,1:T(4,128)S(1)} fusion(bf16[256,4,2,256]{0,1,3,2:T(4,128)(2,1)S(1)} %copy.57, bf16[256,4,2,256,1]{3,0,2,1,4:T(8,128)(2,1)S(1)} %fusion.1), kind=kOutput, calls=%fused_computation.11 | convolution fusion | flops 8388608 | bytes 2097408 | tf_op jit(solution)/shard_map/dot_general | solution.py:27
  95.5 0.1 multiply_reduce_fusion.3
  95.6 5.2 %all_gather.3 = f32[8,2,8]{2,1,0:T(2,128)S(1)} all-gather(f32[2,2,8]{2,1,0:T(2,128)S(1)} %pad_maximum_fusion.12), channel_id=1, replica_groups=mesh['src'=8,'snk'=4] {'snk'}, dimensions={0}, use_global_device_ids=true | all-gather | bytes 640 | tf_op jit(solution)/shard_map/all_gather | solution.py:86
  100.9 0.6 gather_fusion.1
  101.4 0.7 fusion.31
  (27 shorter events, 0.4 us)
Async XLA Ops:
  0.0 6.3 %copy-start.5 = (s32[8,8]{1,0:T(8,128)S(1)}, s32[8,8]{1,0:T(8,128)}, u32[]{:S(2)}) copy-start(s32[8,8]{1,0:T(8,128)} %param.8) | copy-start | bytes 772
  0.0 6.3 %copy-start.7 = (s32[4]{0:T(128)S(1)}, s32[4]{0:T(128)}, u32[]{:S(2)}) copy-start(s32[4]{0:T(128)} %param.11) | copy-start | bytes 52
  2.0 16.0 %all-to-all-start.1 = ((bf16[2,4,2,64,256]{4,3,2,0,1:T(8,128)(2,1)}), bf16[2,4,2,64,256]{4,3,2,0,1:T(8,128)(2,1)S(1)}, u32[]{:S(2)}, u32[]{:S(2)}) async-start(bf16[2,4,2,64,256]{4,3,2,0,1:T(8,128)(2,1)} %copy.52), calls=%async_computation.1 | async-start | bytes 1048576 | tf_op jit(solution)/shard_map/all_to_all | solution.py:78
  16.7 1.3 %copy-start = (bf16[8,32,2,1,8,256]{5,1,2,4,3,0:T(8,128)(2,1)}, bf16[8,32,2,1,8,256]{5,1,2,4,3,0:T(8,128)(2,1)S(1)}, u32[]{:S(2)}) copy-start(bf16[8,32,2,1,8,256]{5,1,2,4,3,0:T(8,128)(2,1)S(1)} %fusion.23) | copy-start | bytes 6291460
  18.0 6.7 %copy-start.6 = (s32[1,8,3]{1,0,2:T(1,128)S(1)}, s32[1,8,3]{1,0,2:T(1,128)}, u32[]{:S(2)}) copy-start(s32[1,8,3]{1,0,2:T(1,128)} %param.9) | copy-start | bytes 292
  18.0 8.0 %copy-start.8 = (s32[16]{0:T(128)S(1)}, s32[16]{0:T(128)}, u32[]{:S(2)}) copy-start(s32[16]{0:T(128)} %param.10) | copy-start | bytes 196
  18.0 55.5 %all-to-all-start = ((bf16[8,32,2,1,8,256]{5,1,2,4,3,0:T(8,128)(2,1)}), bf16[8,32,2,1,8,256]{5,1,2,4,3,0:T(8,128)(2,1)S(1)}, u32[]{:S(2)}, u32[]{:S(2)}) async-start(bf16[8,32,2,1,8,256]{5,1,2,4,3,0:T(8,128)(2,1)} %copy-done), calls=%async_computation | async-start | bytes 4194304 | tf_op jit(solution)/shard_map/all_to_all | solution.py:67
  73.8 1.3 %copy-start.1 = (bf16[8,32,2,1,8,256]{5,1,0,2,4,3:T(8,128)(2,1)}, bf16[8,32,2,1,8,256]{5,1,0,2,4,3:T(8,128)(2,1)S(1)}, u32[]{:S(2)}) copy-start(bf16[8,32,2,1,8,256]{5,1,0,2,4,3:T(8,128)(2,1)S(1)} %copy.51) | copy-start | bytes 6291460
  76.8 1.9 %copy-start.2 = (bf16[8,32,2,1,8,256]{5,1,0,2,4,3:T(8,128)(2,1)S(1)}, bf16[8,32,2,1,8,256]{5,1,0,2,4,3:T(8,128)(2,1)}, u32[]{:S(2)}) copy-start(bf16[8,32,2,1,8,256]{5,1,0,2,4,3:T(8,128)(2,1)} %copy-done.1) | copy-start | bytes 6291460
  80.5 5.0 %copy-start.3 = (bf16[1,2,256,256]{3,2,1,0:T(8,128)(2,1)S(1)}, bf16[1,2,256,256]{3,2,1,0:T(8,128)(2,1)}, u32[]{:S(2)}) copy-start(bf16[1,2,256,256]{3,2,1,0:T(8,128)(2,1)} %get-tuple-element.49) | copy-start | bytes 786436
  80.5 5.0 %copy-start.4 = (bf16[1,2,256,256]{3,2,1,0:T(8,128)(2,1)S(1)}, bf16[1,2,256,256]{3,2,1,0:T(8,128)(2,1)}, u32[]{:S(2)}) copy-start(bf16[1,2,256,256]{3,2,1,0:T(8,128)(2,1)} %get-tuple-element.50) | copy-start | bytes 786436
